TPU v7x, 32 devices: a whole 2x2x4 slice. The times are simulated.
32 devices in a mesh: band: 4 (over y, x), dom: 8 (over z, core).
Axes of the slice: x: 2, y: 2, z: 4, core: 2. Of those that a mesh axis runs over, the one named last changes fastest.
Arguments:
- orbitals: float32 [1024, 32768], P('band', 'dom'), may hold values from -6 to 6
- projectors: float32 [256, 512, 128], P('dom'), may hold values from -0.25 to 0.25
- window_start: int32 [256], P('dom'), may hold values from 0 to 3584
- slot_atom: int32 [8, 32], replicated, may hold values from 0 to 23, as said below
- atom_home: int32 [24], replicated, may hold values from 0 to 23, as said below
- atom_matrices: float32 [24, 128, 128], P('dom'), may hold values from -0.1875 to 0.1875
- rotation: float32 [1024, 1024], P('band'), may hold values from -0.1875 to 0.1875
Outputs:
- rotated: float32 [1024, 32768], P('band', 'dom')
Inputs may be any that keep to these rules, and one draw needn't show every extreme that they name: `atom_home`: a permutation; atom a is owned by domain atom_home[a] // 3, so every domain owns 3 atoms. `slot_atom`: in one domain at most 8 windows have atoms of one owner; in every domain some owner has exactly 8 of them, and some owner has exactly 8 from every domain.
All inputs are finite; a program needn't handle non-finite values.
Results may differ from a plain program's by a relative error of at most 0.0003.
Values sent between devices are 32-bit elements; how exact they have to be, the bound alone decides.
No kernel may reach another device: no remote copies, remote signals or barrier semaphores. Data moves between devices by JAX's collectives and lax.ppermute only.
A program may use at most 128 MiB of HBM per device.

v0:
```python
import jax
import jax.numpy as jnp
from jax import lax
from jax.sharding import PartitionSpec as P

HIGHEST = lax.Precision.HIGHEST


def per_device(orbitals, projectors, window_start, slot_atom, atom_home, atom_matrices, rotation):
    own_domain = lax.axis_index("dom")
    slot_count = projectors.shape[0]
    window = projectors.shape[1]
    atom_count = atom_home.shape[0]
    columns = rotation
    base_field = jnp.dot(
        columns,
        lax.all_gather(orbitals, "band", axis=0, tiled=True),
        precision=HIGHEST,
        preferred_element_type=jnp.float32,
    )
    windows = jax.vmap(lambda offset: lax.dynamic_slice_in_dim(orbitals, offset, window, 1))(
        window_start
    )
    partials = jnp.einsum("sbw,swp->sbp", windows, projectors, precision=HIGHEST)
    atom_ids = jnp.arange(atom_count, dtype=jnp.int32)
    home_table = jnp.sum(
        jnp.where(slot_atom[:, :, None] == atom_ids[None, None, :], atom_home[None, None, :], 0),
        axis=2,
    )
    own_home = lax.dynamic_index_in_dim(home_table, own_domain, 0, keepdims=False)
    home_match = (atom_ids[:, None] == own_home[None, :]).astype(jnp.float32)
    per_atom = jnp.einsum("rs,sbp->rbp", home_match, partials, precision=HIGHEST)
    owned_sums = lax.psum_scatter(per_atom, "dom", scatter_dimension=0, tiled=True)
    owned_factors = jnp.einsum("abp,apq->abq", owned_sums, atom_matrices, precision=HIGHEST)
    columns = rotation
    owned_factors = jnp.einsum(
        "bc,scp->sbp",
        columns,
        lax.all_gather(owned_factors, "band", axis=1, tiled=True),
        precision=HIGHEST,
    )
    all_factors = lax.all_gather(owned_factors, "dom", axis=0, tiled=True)
    slot_factors = jnp.einsum("rs,rbp->sbp", home_match, all_factors, precision=HIGHEST)
    updates = jnp.einsum("sbq,swq->sbw", slot_factors, projectors, precision=HIGHEST)

    def add_window(slot_index, current):
        offset = window_start[slot_index]
        previous = lax.dynamic_slice_in_dim(current, offset, window, 1)
        return lax.dynamic_update_slice_in_dim(current, previous + updates[slot_index], offset, 1)

    corrected = lax.fori_loop(0, slot_count, add_window, base_field)
    return corrected


def solution(mesh):
    in_specs = (
        P("band", "dom"),
        P("dom", None, None),
        P("dom"),
        P(),
        P(),
        P("dom", None, None),
        P("band", None),
    )
    out_specs = P("band", "dom")
    return jax.shard_map(
        per_device, mesh=mesh, in_specs=in_specs, out_specs=out_specs, check_vma=False
    )
```

profile of v0, /device:TPU:0, one launch (start us, length us, event | category | flops | bytes accessed | tf_op | source)
XLA Modules:
  0.0 689.3 jit_solution(3986818245490201017)
XLA Ops:
  7.3 107.7 %while.15 = (s32[]{:T(128)}, f32[256,4096]{1,0:T(8,128)}, s32[32,2]{0,1:T(2,128)S(1)}, f32[32,256,512]{2,1,0:T(8,128)}, s32[]{:T(128)}) while((s32[]{:T(128)}, f32[256,4096]{1,0:T(8,128)}, s32[32,2]{0,1:T(2,128)S(1)}, f32[32,256,512]{2,1,0:T(8,128)}, s32[]{:T(128)}) %tuple.39), condition=%wide.while_cond, body=%wide.while_body.sunk | while | flops 2 | bytes 1049689 | solution.py:21
  115.1 19.3 %fusion.14 = f32[32,256,128]{2,1,0:T(8,128)S(1)} fusion(f32[32,256,512]{2,1,0:T(8,128)} %get-tuple-element.92, f32[32,512,128]{2,1,0:T(8,128)} %param.10), kind=kOutput, calls=%fused_computation.21 | convolution fusion | flops 6442450944 | bytes 29360128 | tf_op jit(solution)/shard_map/sbw,swp->sbp/dot_general | solution.py:24
  134.4 4.3 fusion.2
  141.0 43.3 %reduce-scatter.2.cloned.1.call-done = f32[3,256,128]{2,1,0:T(8,128)} async-done(((f32[24,256,128]{2,1,0:T(8,128)}), f32[3,256,128]{2,1,0:T(8,128)}) %reduce-scatter.2.cloned.1.call-update) | async-done | bytes 393232 | tf_op jit(solution)/shard_map/reduce_scatter | solution.py:33
  186.7 30.0 %all-gather.6.cloned.1.call-done = f32[3,1024,128]{2,1,0:T(8,128)} async-done(((f32[3,256,128]{2,1,0:T(8,128)}), f32[3,1024,128]{2,1,0:T(8,128)}) %all-gather.6.cloned.1.call-update) | async-done | bytes 1572880 | tf_op jit(solution)/shard_map/all_gather | solution.py:39
  216.7 4.0 convolution_bitcast_fusion
  222.3 37.8 %all-gather.8.cloned.1.call-done = f32[24,256,128]{2,1,0:T(8,128)} async-done(((f32[3,256,128]{2,1,0:T(8,128)}), f32[24,256,128]{2,1,0:T(8,128)}) %all-gather.8.cloned.1.call-update) | async-done | bytes 3145744 | tf_op jit(solution)/shard_map/all_gather | solution.py:42
  260.1 5.8 fusion.4
  265.9 21.7 %fusion = f32[32,256,512]{2,1,0:T(8,128)} fusion(f32[32,512,128]{2,1,0:T(8,128)} %param.10, f32[32,256,128]{2,0,1:T(8,128)S(1)} %fusion.4), kind=kOutput, calls=%fused_computation.3 | convolution fusion | flops 6442450944 | bytes 29360128 | tf_op jit(solution)/shard_map/sbq,swq->sbw/dot_general | solution.py:44
  287.6 130.4 %all-gather.4.cloned.1.call-done = f32[1024,4096]{1,0:T(8,128)} async-done(((f32[256,4096]{1,0:T(8,128)}), f32[1024,4096]{1,0:T(8,128)}) %all-gather.4.cloned.1.call-update) | async-done | bytes 16777232 | tf_op jit(solution)/shard_map/all_gather | solution.py:17
  418.0 18.0 %fusion.13 = f32[256,4096]{1,0:T(8,128)} fusion(f32[256,1024]{1,0:T(8,128)S(1)} %copy-done, f32[1024,4096]{1,0:T(8,128)} %all-gather.4.cloned.1.call-done), kind=kOutput, calls=%fused_computation.20 | convolution fusion | flops 12884901888 | bytes 22020096 | tf_op jit(solution)/shard_map/dot_general | solution.py:15
  436.0 246.8 %while.14 = (s32[]{:T(128)}, f32[256,4096]{1,0:T(8,128)}, s32[32]{0:T(128)S(1)}, f32[32,256,512]{2,1,0:T(8,128)}, s32[]{:T(128)}, /*index=5*/s32[]{:T(128)}, s32[]{:T(128)}) while((s32[]{:T(128)}, f32[256,4096]{1,0:T(8,128)}, s32[32]{0:T(128)S(1)}, f32[32,256,512]{2,1,0:T(8,128)}, s32[]{:T(128)}, /*index=5*/s32[]{:T(128)}, s32[]{:T(128)}) %tuple.53), condition=%wide.region_3.4_spmd, body=%wide.region_2.3_spmd.sunk | while | flops 131077 | bytes 2621575 | solution.py:51
  439.9 3.8 dynamic_update_slice.8
  447.6 3.8 dynamic_update_slice.8
  455.4 3.8 dynamic_update_slice.8
  463.1 3.8 dynamic_update_slice.8
  470.8 3.8 dynamic_update_slice.8
  478.5 3.8 dynamic_update_slice.8
  486.2 3.8 dynamic_update_slice.8
  509.2 3.8 dynamic_update_slice.8
  516.9 3.8 dynamic_update_slice.8
  524.6 3.8 dynamic_update_slice.8
  532.3 3.8 dynamic_update_slice.8
  540.1 3.8 dynamic_update_slice.8
  547.8 3.8 dynamic_update_slice.8
  555.5 3.8 dynamic_update_slice.8
  563.2 3.8 dynamic_update_slice.8
  570.9 3.8 dynamic_update_slice.8
  578.6 3.8 dynamic_update_slice.8
  586.4 3.8 dynamic_update_slice.8
  609.5 3.8 dynamic_update_slice.8
  617.2 3.8 dynamic_update_slice.8
  (198 shorter events, 226.6 us)
Async XLA Ops:
  6.5 210.2 %copy-start = (f32[256,1024]{1,0:T(8,128)S(1)}, f32[256,1024]{1,0:T(8,128)}, u32[]{:S(2)}) copy-start(f32[256,1024]{1,0:T(8,128)} %param.15) | copy-start | bytes 3145732
  6.5 108.5 %copy-start.2 = (s32[8,32]{1,0:T(8,128)S(1)}, s32[8,32]{1,0:T(8,128)}, u32[]{:S(2)}) copy-start(s32[8,32]{1,0:T(8,128)} %param.12) | copy-start | bytes 3076
  6.5 108.5 %copy-start.3 = (s32[24]{0:T(128)S(1)}, s32[24]{0:T(128)}, u32[]{:S(2)}) copy-start(s32[24]{0:T(128)} %param.13) | copy-start | bytes 292
  6.5 177.7 %reduce-scatter.2.cloned.1.call-start = ((), (), s32[]{:S(2)}) async-start(), calls=%async_computation.2 | async-start | bytes 3538944 | tf_op jit(solution)/shard_map/reduce_scatter | solution.py:33
  138.7 45.6 %copy-start.1 = (f32[3,128,128]{2,1,0:T(8,128)S(1)}, f32[3,128,128]{2,1,0:T(8,128)}, u32[]{:S(2)}) copy-start(f32[3,128,128]{2,1,0:T(8,128)} %param.14) | copy-start | bytes 589828
  140.9 75.8 %all-gather.6.cloned.1.call-start = ((), (), s32[]{:S(2)}) async-start(), calls=%async_computation.3 | async-start | bytes 1966080 | tf_op jit(solution)/shard_map/all_gather | solution.py:39
  186.5 73.6 %all-gather.8.cloned.1.call-start = ((), (), s32[]{:S(2)}) async-start(), calls=%async_computation.4 | async-start | bytes 3538944 | tf_op jit(solution)/shard_map/all_gather | solution.py:42
  221.7 196.3 %all-gather.4.cloned.1.call-start = ((), (), s32[]{:S(2)}) async-start(), calls=%async_computation.1 | async-start | bytes 20971520 | tf_op jit(solution)/shard_map/all_gather | solution.py:17
  287.6 148.4 %copy-start.4 = (s32[32]{0:T(128)S(1)}, s32[32]{0:T(128)}, u32[]{:S(2)}) copy-start(s32[32]{0:T(128)} %param.11) | copy-start | bytes 388
Sparse Core Ops, SparseCore 0:
  141.1 43.1 reduce-scatter.1
  186.6 30.0 all-gather.5
  221.8 38.2 all-gather.7
  261.8 156.1 all-gather.3
where the time goes:
time: 695 us; the launch traced here: 689 us
  local copies, waits for them, and re-layouts  251 us (36%)
  waiting for transfers between devices  242 us (35%)
  matrix products  75.2 us (11%)
  loops' own time  59.9 us (9%)
  other arithmetic  47.5 us (7%)
  between operations  13.2 us (2%)
    all_gather x1, waiting for transfers between devices, per_device(): lax.all_gather(orbitals, 'band', axis=0, tiled=True)  130 us
    dynamic_update_slice x32, local copies, waits for them, and re-layouts, add_window(): lax.dynamic_update_slice_in_dim(current, previous + updates[slot_index],...  120 us
    gather x96, local copies, waits for them, and re-layouts  108 us
    another operation x1, loops' own time, per_device(): corrected = lax.fori_loop(0, slot_count, add_window, base_field)  59.9 us
    add x32, other arithmetic, add_window(): previous + updates[slot_index]  46.6 us
    reduce_scatter x1, waiting for transfers between devices, per_device(): lax.psum_scatter(per_atom, 'dom', scatter_dimension=0, tiled=True)  43.3 us
    all_gather x1, waiting for transfers between devices, per_device(): all_factors = lax.all_gather(owned_factors, 'dom', axis=0, tiled=True)  37.8 us
    all_gather x1, waiting for transfers between devices, per_device(): lax.all_gather(owned_factors, 'band', axis=1, tiled=True)  30 us
  transfers between devices with their start and end apart: 4, of which 4 were waited for; matrix products, arithmetic and copies ran while one was open for 4% of the time, Pallas kernels for 0%

commit v1 on v0

--- a/solution.py
+++ b/solution.py
@@ -4,6 +4,17 @@
 from jax.sharding import PartitionSpec as P
 
 HIGHEST = lax.Precision.HIGHEST
+
+
+def around_the_ring(value, axis, dim):
+    peers = lax.axis_size(axis)
+    right = [(i, (i + 1) % peers) for i in range(peers)]
+    parts = [value]
+    for far in range(1, peers):
+        parts = [lax.ppermute(parts[0], axis, right), *parts]
+    result = jnp.concatenate(parts, axis=dim)
+    shift = (lax.axis_index(axis) + 1) * parts[-1].shape[dim]
+    return jnp.roll(result, shift, axis=dim)
 
 
 def per_device(orbitals, projectors, window_start, slot_atom, atom_home, atom_matrices, rotation):
@@ -39,7 +50,7 @@
         lax.all_gather(owned_factors, "band", axis=1, tiled=True),
         precision=HIGHEST,
     )
-    all_factors = lax.all_gather(owned_factors, "dom", axis=0, tiled=True)
+    all_factors = around_the_ring(owned_factors, "dom", 0)
     slot_factors = jnp.einsum("rs,rbp->sbp", home_match, all_factors, precision=HIGHEST)
     updates = jnp.einsum("sbq,swq->sbw", slot_factors, projectors, precision=HIGHEST)
 

time: 695 us -> 653 us (0.940)
  waiting for transfers between devices: 242 us -> 194 us
  local copies, waits for them, and re-layouts: 251 us -> 259 us
    all_gather x1, waiting for transfers between devices: 130 us -> 57.7 us  [per_device(): lax.all_gather(orbitals, 'band', axis=0, tiled=True)]
    ppermute x0 -> x7, waiting for transfers between devices: none -> 63.4 us  [around_the_ring(): parts = [lax.ppermute(parts[0], axis, right), *parts]]
    all_gather x1 -> x0, waiting for transfers between devices: 37.8 us -> none  [per_device(): all_factors = lax.all_gather(owned_factors, 'dom', axis=0, tiled=True)]
  transfers between devices with their start and end apart: 4 -> 10, of which waited for: 4 -> 10; matrix products, arithmetic and copies ran while one was open for 4% -> 6% of each run, Pallas kernels for 0% -> 0%
where the time goes in v1:
time: 653 us; the launch traced here: 647 us
  local copies, waits for them, and re-layouts  259 us (40%)
  waiting for transfers between devices  194 us (30%)
  matrix products  71.2 us (11%)
  loops' own time  61.2 us (9%)
  other arithmetic  48.2 us (7%)
  between operations  13.3 us (2%)
    dynamic_update_slice x32, local copies, waits for them, and re-layouts, add_window(): lax.dynamic_update_slice_in_dim(current, previous + updates[slot_index],...  120 us
    gather x96, local copies, waits for them, and re-layouts  107 us
    ppermute x7, waiting for transfers between devices, around_the_ring(): parts = [lax.ppermute(parts[0], axis, right), *parts]  63.4 us
    another operation x1, loops' own time, per_device(): corrected = lax.fori_loop(0, slot_count, add_window, base_field)  61.2 us
    all_gather x1, waiting for transfers between devices, per_device(): lax.all_gather(orbitals, 'band', axis=0, tiled=True)  57.7 us
    add x32, other arithmetic, add_window(): previous + updates[slot_index]  46.6 us
    reduce_scatter x1, waiting for transfers between devices, per_device(): lax.psum_scatter(per_atom, 'dom', scatter_dimension=0, tiled=True)  43.3 us
    all_gather x1, waiting for transfers between devices, per_device(): lax.all_gather(owned_factors, 'band', axis=1, tiled=True)  29.4 us
  transfers between devices with their start and end apart: 10, of which 10 were waited for; matrix products, arithmetic and copies ran while one was open for 6% of the time, Pallas kernels for 0%

profile of v1, /device:TPU:0, one launch (start us, length us, event | category | flops | bytes accessed | tf_op | source)
XLA Modules:
  0.0 647.4 jit_solution(543942780862168432)
XLA Ops:
  7.3 107.1 %while.15 = (s32[]{:T(128)}, f32[256,4096]{1,0:T(8,128)}, s32[32,2]{0,1:T(2,128)S(1)}, f32[32,256,512]{2,1,0:T(8,128)}, s32[]{:T(128)}) while((s32[]{:T(128)}, f32[256,4096]{1,0:T(8,128)}, s32[32,2]{0,1:T(2,128)S(1)}, f32[32,256,512]{2,1,0:T(8,128)}, s32[]{:T(128)}) %tuple.39), condition=%wide.while_cond, body=%wide.while_body.sunk | while | flops 2 | bytes 1049689 | solution.py:32
  115.2 19.3 %fusion.13 = f32[32,256,128]{2,1,0:T(8,128)S(1)} fusion(f32[32,256,512]{2,1,0:T(8,128)} %get-tuple-element.92, f32[32,512,128]{2,1,0:T(8,128)} %param.10), kind=kOutput, calls=%fused_computation.37 | convolution fusion | flops 6442450944 | bytes 29360128 | tf_op jit(solution)/shard_map/sbw,swp->sbp/dot_general | solution.py:35
  134.5 4.3 fusion.2
  141.1 43.3 %reduce-scatter.2.cloned.1.call-done = f32[3,256,128]{2,1,0:T(8,128)} async-done(((f32[24,256,128]{2,1,0:T(8,128)}), f32[3,256,128]{2,1,0:T(8,128)}) %reduce-scatter.2.cloned.1.call-update) | async-done | bytes 393232 | tf_op jit(solution)/shard_map/reduce_scatter | solution.py:44
  187.4 29.4 %all-gather.5.cloned.1.call-done = f32[3,1024,128]{1,2,0:T(8,128)} async-done(((f32[3,256,128]{1,2,0:T(8,128)}), f32[3,1024,128]{1,2,0:T(8,128)}) %all-gather.5.cloned.1.call-update) | async-done | bytes 1572880 | tf_op jit(solution)/shard_map/all_gather | solution.py:50
  219.7 9.0 %collective-permute-done = f32[3,256,128]{1,2,0:T(8,128)S(1)} collective-permute-done((f32[3,256,128]{1,2,0:T(8,128)S(1)}, f32[3,256,128]{1,2,0:T(8,128)S(1)}, u32[]{:S(2)}, u32[]{:S(2)}) %collective-permute-start) | collective-permute-done | bytes 393248 | tf_op jit(solution)/shard_map/ppermute | solution.py:14
  228.6 9.0 %collective-permute-done.1 = f32[3,256,128]{1,2,0:T(8,128)S(1)} collective-permute-done((f32[3,256,128]{1,2,0:T(8,128)S(1)}, f32[3,256,128]{1,2,0:T(8,128)S(1)}, u32[]{:S(2)}, u32[]{:S(2)}) %collective-permute-start.1) | collective-permute-done | bytes 393248 | tf_op jit(solution)/shard_map/ppermute | solution.py:14
  237.6 9.0 %collective-permute-done.2 = f32[3,256,128]{1,2,0:T(8,128)S(1)} collective-permute-done((f32[3,256,128]{1,2,0:T(8,128)S(1)}, f32[3,256,128]{1,2,0:T(8,128)S(1)}, u32[]{:S(2)}, u32[]{:S(2)}) %collective-permute-start.2) | collective-permute-done | bytes 393248 | tf_op jit(solution)/shard_map/ppermute | solution.py:14
  246.6 9.0 %collective-permute-done.3 = f32[3,256,128]{1,2,0:T(8,128)S(1)} collective-permute-done((f32[3,256,128]{1,2,0:T(8,128)S(1)}, f32[3,256,128]{1,2,0:T(8,128)S(1)}, u32[]{:S(2)}, u32[]{:S(2)}) %collective-permute-start.3) | collective-permute-done | bytes 393248 | tf_op jit(solution)/shard_map/ppermute | solution.py:14
  255.6 9.0 %collective-permute-done.4 = f32[3,256,128]{1,2,0:T(8,128)S(1)} collective-permute-done((f32[3,256,128]{1,2,0:T(8,128)S(1)}, f32[3,256,128]{1,2,0:T(8,128)S(1)}, u32[]{:S(2)}, u32[]{:S(2)}) %collective-permute-start.4) | collective-permute-done | bytes 393248 | tf_op jit(solution)/shard_map/ppermute | solution.py:14
  264.6 9.1 %collective-permute-done.5 = f32[3,256,128]{1,2,0:T(8,128)} collective-permute-done((f32[3,256,128]{1,2,0:T(8,128)S(1)}, f32[3,256,128]{1,2,0:T(8,128)}, u32[]{:S(2)}, u32[]{:S(2)}) %collective-permute-start.5) | collective-permute-done | bytes 393248 | tf_op jit(solution)/shard_map/ppermute | solution.py:14
  273.7 9.3 %collective-permute-done.6 = f32[3,256,128]{1,2,0:T(8,128)} collective-permute-done((f32[3,256,128]{1,2,0:T(8,128)}, f32[3,256,128]{1,2,0:T(8,128)}, u32[]{:S(2)}, u32[]{:S(2)}) %collective-permute-start.6) | collective-permute-done | bytes 393248 | tf_op jit(solution)/shard_map/ppermute | solution.py:14
  293.6 3.8 fusion.6
  297.4 20.8 %fusion = f32[32,256,512]{2,1,0:T(8,128)} fusion(f32[32,512,128]{2,1,0:T(8,128)} %param.10, f32[32,256,128]{2,0,1:T(8,128)S(1)} %fusion.6), kind=kOutput, calls=%fused_computation.3 | convolution fusion | flops 6442450944 | bytes 29360128 | tf_op jit(solution)/shard_map/sbq,swq->sbw/dot_general | solution.py:55
  318.2 57.7 %all-gather.3.cloned.1.call-done = f32[1024,4096]{1,0:T(8,128)} async-done(((f32[256,4096]{1,0:T(8,128)}), f32[1024,4096]{1,0:T(8,128)}) %all-gather.3.cloned.1.call-update) | async-done | bytes 16777232 | tf_op jit(solution)/shard_map/all_gather | solution.py:28
  375.9 18.0 %fusion.12 = f32[256,4096]{1,0:T(8,128)} fusion(f32[256,1024]{1,0:T(8,128)S(1)} %copy-done, f32[1024,4096]{1,0:T(8,128)} %all-gather.3.cloned.1.call-done), kind=kOutput, calls=%fused_computation.36 | convolution fusion | flops 12884901888 | bytes 22020096 | tf_op jit(solution)/shard_map/dot_general | solution.py:26
  393.9 247.0 %while.14 = (s32[]{:T(128)}, f32[256,4096]{1,0:T(8,128)}, s32[32]{0:T(128)S(1)}, f32[32,256,512]{2,1,0:T(8,128)}, s32[]{:T(128)}, /*index=5*/s32[]{:T(128)}, s32[]{:T(128)}) while((s32[]{:T(128)}, f32[256,4096]{1,0:T(8,128)}, s32[32]{0:T(128)S(1)}, f32[32,256,512]{2,1,0:T(8,128)}, s32[]{:T(128)}, /*index=5*/s32[]{:T(128)}, s32[]{:T(128)}) %tuple.51), condition=%wide.region_3.4_spmd, body=%wide.region_2.3_spmd.sunk | while | flops 131077 | bytes 2621575 | solution.py:62
  397.8 3.8 dynamic_update_slice.8
  405.6 3.8 dynamic_update_slice.8
  413.3 3.8 dynamic_update_slice.8
  421.0 3.8 dynamic_update_slice.8
  428.7 3.8 dynamic_update_slice.8
  436.5 3.8 dynamic_update_slice.8
  444.2 3.8 dynamic_update_slice.8
  467.2 3.8 dynamic_update_slice.8
  474.9 3.8 dynamic_update_slice.8
  482.6 3.8 dynamic_update_slice.8
  490.3 3.8 dynamic_update_slice.8
  498.1 3.8 dynamic_update_slice.8
  513.5 3.8 dynamic_update_slice.8
  529.0 3.8 dynamic_update_slice.8
  544.4 3.8 dynamic_update_slice.8
  (222 shorter events, 256.7 us)
Async XLA Ops:
  6.5 210.2 %copy-start = (f32[256,1024]{1,0:T(8,128)S(1)}, f32[256,1024]{1,0:T(8,128)}, u32[]{:S(2)}) copy-start(f32[256,1024]{1,0:T(8,128)} %param.15) | copy-start | bytes 3145732
  6.5 177.8 %reduce-scatter.2.cloned.1.call-start = ((), (), s32[]{:S(2)}) async-start(), calls=%async_computation.2 | async-start | bytes 3538944 | tf_op jit(solution)/shard_map/reduce_scatter | solution.py:44
  138.8 45.6 %copy-start.1 = (f32[3,128,128]{2,1,0:T(8,128)S(1)}, f32[3,128,128]{2,1,0:T(8,128)}, u32[]{:S(2)}) copy-start(f32[3,128,128]{2,1,0:T(8,128)} %param.14) | copy-start | bytes 589828
  141.0 75.7 %all-gather.5.cloned.1.call-start = ((), (), s32[]{:S(2)}) async-start(), calls=%async_computation.3 | async-start | bytes 1966080 | tf_op jit(solution)/shard_map/all_gather | solution.py:50
  186.6 189.3 %all-gather.3.cloned.1.call-start = ((), (), s32[]{:S(2)}) async-start(), calls=%async_computation.1 | async-start | bytes 20971520 | tf_op jit(solution)/shard_map/all_gather | solution.py:28
  219.6 9.1 %collective-permute-start = (f32[3,256,128]{1,2,0:T(8,128)S(1)}, f32[3,256,128]{1,2,0:T(8,128)S(1)}, u32[]{:S(2)}, u32[]{:S(2)}) collective-permute-start(f32[3,256,128]{1,2,0:T(8,128)S(1)} %convolution_bitcast_fusion), channel_id=1, source_target_pairs={{0,1},{1,2},{2,3},{3,4},{4,5},{5,6},{6,7},{7,0},{8,9},{9,10},{10,1... | collective-permute-start | bytes 1179656 | tf_op jit(solution)/shard_map/ppermute | solution.py:14
  228.6 9.0 %collective-permute-start.1 = (f32[3,256,128]{1,2,0:T(8,128)S(1)}, f32[3,256,128]{1,2,0:T(8,128)S(1)}, u32[]{:S(2)}, u32[]{:S(2)}) collective-permute-start(f32[3,256,128]{1,2,0:T(8,128)S(1)} %collective-permute-done), channel_id=1, source_target_pairs={{0,1},{1,2},{2,3},{3,4},{4,5},{5,6},{6,7},{7,0},{8,9},{9,10},{10,1... | collective-permute-start | bytes 1179656 | tf_op jit(solution)/shard_map/ppermute | solution.py:14
  237.6 9.0 %collective-permute-start.2 = (f32[3,256,128]{1,2,0:T(8,128)S(1)}, f32[3,256,128]{1,2,0:T(8,128)S(1)}, u32[]{:S(2)}, u32[]{:S(2)}) collective-permute-start(f32[3,256,128]{1,2,0:T(8,128)S(1)} %collective-permute-done.1), channel_id=1, source_target_pairs={{0,1},{1,2},{2,3},{3,4},{4,5},{5,6},{6,7},{7,0},{8,9},{9,10},{10,1... | collective-permute-start | bytes 1179656 | tf_op jit(solution)/shard_map/ppermute | solution.py:14
  246.6 9.0 %collective-permute-start.3 = (f32[3,256,128]{1,2,0:T(8,128)S(1)}, f32[3,256,128]{1,2,0:T(8,128)S(1)}, u32[]{:S(2)}, u32[]{:S(2)}) collective-permute-start(f32[3,256,128]{1,2,0:T(8,128)S(1)} %collective-permute-done.2), channel_id=1, source_target_pairs={{0,1},{1,2},{2,3},{3,4},{4,5},{5,6},{6,7},{7,0},{8,9},{9,10},{10,1... | collective-permute-start | bytes 1179656 | tf_op jit(solution)/shard_map/ppermute | solution.py:14
  255.6 9.0 %collective-permute-start.4 = (f32[3,256,128]{1,2,0:T(8,128)S(1)}, f32[3,256,128]{1,2,0:T(8,128)S(1)}, u32[]{:S(2)}, u32[]{:S(2)}) collective-permute-start(f32[3,256,128]{1,2,0:T(8,128)S(1)} %collective-permute-done.3), channel_id=1, source_target_pairs={{0,1},{1,2},{2,3},{3,4},{4,5},{5,6},{6,7},{7,0},{8,9},{9,10},{10,1... | collective-permute-start | bytes 1179656 | tf_op jit(solution)/shard_map/ppermute | solution.py:14
  264.6 9.1 %collective-permute-start.5 = (f32[3,256,128]{1,2,0:T(8,128)S(1)}, f32[3,256,128]{1,2,0:T(8,128)}, u32[]{:S(2)}, u32[]{:S(2)}) collective-permute-start(f32[3,256,128]{1,2,0:T(8,128)S(1)} %collective-permute-done.4), channel_id=1, source_target_pairs={{0,1},{1,2},{2,3},{3,4},{4,5},{5,6},{6,7},{7,0},{8,9},{9,10},{10,1... | collective-permute-start | bytes 1179656 | tf_op jit(solution)/shard_map/ppermute | solution.py:14
  273.7 9.3 %collective-permute-start.6 = (f32[3,256,128]{1,2,0:T(8,128)}, f32[3,256,128]{1,2,0:T(8,128)}, u32[]{:S(2)}, u32[]{:S(2)}) collective-permute-start(f32[3,256,128]{1,2,0:T(8,128)} %collective-permute-done.5), channel_id=1, source_target_pairs={{0,1},{1,2},{2,3},{3,4},{4,5},{5,6},{6,7},{7,0},{8,9},{9,10},{10,1... | collective-permute-start | bytes 1179656 | tf_op jit(solution)/shard_map/ppermute | solution.py:14
  318.2 75.7 %copy-start.2 = (s32[32]{0:T(128)S(1)}, s32[32]{0:T(128)}, u32[]{:S(2)}) copy-start(s32[32]{0:T(128)} %param.11) | copy-start | bytes 388
Sparse Core Ops, SparseCore 0:
  141.1 43.1 reduce-scatter.1
  186.8 29.9 all-gather.4
  218.6 157.2 all-gather.2
